TPU v7x, 256 devices: a whole 4x4x8 slice. The times are simulated.
256 devices in a mesh: orow: 16 (over z_lo, x), ocol: 16 (over z_hi, y, core).
Axes of the slice: x: 4, y: 4, z: 8 (z_hi: 2, z_lo: 4; z = z_hi * 4 + z_lo), core: 2. Of those that a mesh axis runs over, the one named last changes fastest.
Arguments:
- amplitudes: bfloat16 [16, 16, 512, 512], P('orow', 'ocol'), may hold values from -6 to 6
- tile_mask: int32 [16, 16, 2, 2], P('orow', 'ocol'), may hold values 0 or 1
- domain_tiles: int32 [16, 16, 2], replicated, may hold values from 0 to 7, as said below
- cholesky: bfloat16 [16, 2048, 2048], P('ocol'), as said below
Outputs:
- ladder_sym: float32 [16, 16, 512, 512], P('orow', 'ocol')
Inputs may be any that keep to these rules, and one draw needn't show every extreme that they name: `domain_tiles`: for every pair the 2 tile numbers differ, and pair (j, i) lists the same tiles in the same order as pair (i, j). Every vector cholesky[q] is a symmetric 2048 x 2048 matrix.
All inputs are finite; a program needn't handle non-finite values. No bound on the sum of `tile_mask` on one device may be relied on, other than what follows from the above.
Results may differ from a plain program's by a relative error of at most 0.0029.
Values may be sent and summed in bfloat16 or wider, within the bound.
A program may use at most 128 MiB of HBM per device.

v0:
```python
import jax
import jax.numpy as jnp
from jax import lax
from jax.sharding import PartitionSpec as P

TILE = 256
K = 2


def pick_tiles(local_factor, chosen):
    number = local_factor.shape[0]
    tiles = local_factor.shape[1] // TILE
    blocked = local_factor.reshape(number, tiles, TILE, tiles, TILE)
    picked = blocked[:, chosen[..., :, None], :, chosen[..., None, :], :]
    leading = chosen.ndim - 1
    permuted = tuple(range(leading)) + (leading + 2, leading, leading + 3, leading + 1, leading + 4)
    width = chosen.shape[-1] * TILE
    return picked.transpose(permuted).reshape(chosen.shape[:-1] + (number, width, width))


def masked(amplitudes, tile_mask):
    row_pairs = amplitudes.shape[0]
    col_pairs = amplitudes.shape[1]
    shaped = amplitudes.reshape(row_pairs, col_pairs, K, TILE, K, TILE)
    weights = tile_mask.astype(jnp.bfloat16)[:, :, :, None, :, None]
    return (shaped * weights).reshape(amplitudes.shape)


def shards(amplitudes, tile_mask, domain_tiles, cholesky):
    row_pairs = amplitudes.shape[0]
    row_domains = lax.dynamic_slice_in_dim(
        domain_tiles, lax.axis_index("orow") * row_pairs, row_pairs, 0
    )
    weighted = masked(amplitudes, tile_mask)
    gathered = lax.all_gather(weighted, "ocol", axis=1, tiled=True)
    factor = pick_tiles(cholesky, row_domains)
    inner = jnp.einsum(
        "ijqac,ijcd->ijqad", factor, gathered, preferred_element_type=jnp.float32
    ).astype(jnp.bfloat16)
    summed = lax.psum_scatter(
        jnp.einsum("ijqad,ijqbd->jiab", inner, factor, preferred_element_type=jnp.float32),
        "ocol",
        scatter_dimension=0,
        tiled=True,
    )
    ladder = summed.transpose(1, 0, 2, 3)
    turned = lax.all_to_all(ladder, "ocol", split_axis=2, concat_axis=1, tiled=True)
    turned = lax.all_to_all(
        lax.all_to_all(turned, "orow", split_axis=1, concat_axis=0, tiled=True),
        "ocol",
        split_axis=0,
        concat_axis=2,
        tiled=True,
    )
    return ladder + turned.transpose(1, 0, 3, 2)


def solution(mesh):
    return jax.shard_map(
        shards,
        mesh=mesh,
        in_specs=(
            P("orow", "ocol", None, None),
            P("orow", "ocol", None, None),
            P(),
            P("ocol", None, None),
        ),
        out_specs=P("orow", "ocol", None, None),
        check_vma=False,
    )
```

profile of v0, /device:TPU:5, one launch (start us, length us, event | category | flops | bytes accessed | tf_op | source)
XLA Modules:
  0.0 464.3 jit_solution(741445048212051335)
XLA Ops:
  6.5 0.7 convert_bitcast_fusion
  7.2 0.3 mul.16
  7.6 0.3 mul.17
  7.9 1.9 bitcast_multiply_fusion
  9.8 0.0 all-gather.2.cloned.1.call-update
  9.8 0.0 reduce-scatter.2.cloned.1.call-start
  9.9 0.7 compare_select_fusion
  10.6 0.1 copy.29
  10.7 0.1 reshape.87
  10.8 10.3 %copy.40 = bf16[256,8,8,256]{3,2,1,0:T(8,128)(2,1)} copy(bf16[256,8,8,256]{3,1,2,0:T(8,128)(2,1)} %bitcast.45) | data formatting | bytes 16777216
  21.1 8.8 %copy.30 = bf16[8,256,8,256]{3,1,2,0:T(8,128)(2,1)} copy(bf16[8,256,8,256]{3,2,1,0:T(8,128)(2,1)} %bitcast.44) | data formatting | bytes 16777216 | tf_op jit(solution)/shard_map/reshape | solution.py:13
  29.9 9.4 %gather_fusion = bf16[64,256,256]{2,1,0:T(8,128)(2,1)} fusion(bf16[8,256,8,256]{3,1,2,0:T(8,128)(2,1)} %copy.30, s32[64]{0:T(128)S(1)} %reshape.87), kind=kCustom, calls=%fused_computation | custom fusion | bytes 16777728 | tf_op jit(solution)/shard_map/gather | solution.py:14
  39.3 16.3 %copy.31 = bf16[1,16,1,2,256,2,256]{6,5,4,3,1,2,0:T(2,128)(2,1)} copy(bf16[1,16,1,2,256,2,256]{6,4,5,3,1,2,0:T(8,128)(2,1)} %bitcast.43) | data formatting | bytes 16777216 | tf_op jit(solution)/shard_map/transpose | solution.py:18
  55.6 14.2 %reshape.81 = bf16[16,512,512]{2,1,0:T(8,128)(2,1)} reshape(bf16[1,16,1,2,256,2,256]{6,5,4,3,1,2,0:T(2,128)(2,1)} %copy.31) | data formatting | bytes 16777216 | tf_op jit(solution)/shard_map/reshape.10
  69.8 51.9 %all-gather.2.cloned.1.call-done = bf16[1,16,512,512]{3,2,0,1:T(8,128)(2,1)} async-done(((bf16[1,1,512,512]{3,2,0,1:T(8,128)(2,1)}), bf16[1,16,512,512]{3,2,0,1:T(8,128)(2,1)}) %all-gather.2.cloned.1.call-update) | async-done | bytes 8388624 | tf_op jit(solution)/shard_map/all_gather | solution.py:35
  121.8 22.0 %convolution_bitcast_fusion = f32[16,1,512,512]{3,2,0,1:T(8,128)} fusion(bf16[16,512,512]{2,1,0:T(8,128)(2,1)} %reshape.81, bf16[1,16,512,512]{3,2,0,1:T(8,128)(2,1)} %all-gather.2.cloned.1.call-done), kind=kOutput, calls=%fused_computation.1 | convolution fusion | flops 8594128896 | bytes 33554432 | tf_op jit(solution)/shard_map/ijqad,ijqbd->jiab/dot_general | solution.py:41
  143.7 204.4 %reduce-scatter.2.cloned.1.call-done = f32[1,1,512,512]{3,2,0,1:T(8,128)} async-done(((f32[16,1,512,512]{3,2,0,1:T(8,128)}), f32[1,1,512,512]{3,2,0,1:T(8,128)}) %reduce-scatter.2.cloned.1.call-update) | async-done | bytes 1048592 | tf_op jit(solution)/shard_map/reduce_scatter | solution.py:40
  348.1 2.4 copy.33
  350.5 30.4 %all_to_all.36 = f32[1,1,512,512]{3,0,1,2:T(1,128)S(1)} all-to-all(f32[1,1,512,512]{3,0,1,2:T(1,128)S(1)} %copy.33), channel_id=1, replica_groups=mesh['orow'=16,'ocol'=16] {'ocol'}, dimensions={2} | all-to-all | bytes 2097152 | tf_op jit(solution)/shard_map/all_to_all | solution.py:47
  380.9 0.1 copy.34
  381.0 41.7 %all_to_all.37 = f32[1,16,32,512]{3,2,0,1:T(8,128)S(1)} all-to-all(f32[1,16,32,512]{3,2,0,1:T(8,128)S(1)} %copy.34), channel_id=1, replica_groups=mesh['orow'=16,'ocol'=16] {'orow'}, dimensions={1} | all-to-all | bytes 2097152 | tf_op jit(solution)/shard_map/all_to_all | solution.py:49
  422.6 33.2 %all_to_all.38 = f32[16,1,32,512]{3,2,1,0:T(8,128)S(1)} all-to-all(f32[16,1,32,512]{3,2,1,0:T(8,128)S(1)} %bitcast.47), channel_id=1, replica_groups=mesh['orow'=16,'ocol'=16] {'ocol'}, dimensions={0} | all-to-all | bytes 2097152 | tf_op jit(solution)/shard_map/all_to_all | solution.py:48
  455.9 0.3 copy.36
  456.2 1.2 fusion.7
  (9 shorter events, 0.1 us)
Async XLA Ops:
  6.5 115.2 %all-gather.2.cloned.1.call-start = ((), (), s32[]{:S(2)}) async-start(), calls=%async_computation.4 | async-start | bytes 8912896 | tf_op jit(solution)/shard_map/all_gather | solution.py:35
  9.8 338.3 %reduce-scatter.2.cloned.1.call-start = ((), (), s32[]{:S(2)}) async-start(), calls=%async_computation.5 | async-start | bytes 17825792 | tf_op jit(solution)/shard_map/reduce_scatter | solution.py:40
  348.1 108.1 %copy-start = (f32[1,1,512,512]{3,2,0,1:T(8,128)S(1)}, f32[1,1,512,512]{3,2,0,1:T(8,128)}, u32[]{:S(2)}) copy-start(f32[1,1,512,512]{3,2,0,1:T(8,128)} %reduce-scatter.2.cloned.1.call-done) | copy-start | bytes 3145732
Sparse Core Ops, SparseCore 0:
  10.1 111.6 all-gather.1
  143.9 204.2 reduce-scatter.1
where the time goes:
time: 468 us; the launch traced here: 464 us
  waiting for transfers between devices  256 us (55%)
  blocking collectives  105 us (22%)
  local copies, waits for them, and re-layouts  62.7 us (13%)
  matrix products  22 us (5%)
  between operations  13.5 us (3%)
    reduce_scatter x1, waiting for transfers between devices, shards(): lax.psum_scatter(jnp.einsum('ijqad,ijqbd->jiab', inner, factor, preferred...  204 us
    all_gather x1, waiting for transfers between devices, shards(): gathered = lax.all_gather(weighted, 'ocol', axis=1, tiled=True)  51.9 us
    all_to_all x1, blocking collectives, shards(): lax.all_to_all(turned, 'orow', split_axis=1, concat_axis=0, tiled=True)  41.7 us
    all_to_all x1, blocking collectives, shards(): lax.all_to_all(lax.all_to_all(turned, 'orow', split_axis=1, concat_axis=0...  33.2 us
    all_to_all x1, blocking collectives, shards(): lax.all_to_all(ladder, 'ocol', split_axis=2, concat_axis=1, tiled=True)  30.4 us
    dot_general x1, matrix products, shards(): jnp.einsum('ijqad,ijqbd->jiab', inner, factor, preferred_element_type=jnp...  22 us
    transpose x1, local copies, waits for them, and re-layouts, pick_tiles(): picked.transpose(permuted)  16.3 us
    another operation x1, local copies, waits for them, and re-layouts  14.2 us
  transfers between devices with their start and end apart: 2, of which 2 were waited for; matrix products, arithmetic and copies ran while one was open for 13% of the time, Pallas kernels for 0%

commit v1 on v0

v1 whole, which is shorter than its diff:
```python
import functools

import jax
import jax.numpy as jnp
from jax import lax
from jax.experimental import pallas as pl
from jax.experimental.pallas import tpu as pltpu
from jax.sharding import PartitionSpec as P

TILE = 256
DV = 512
NO = 16
RING = 8
PARTS = ((0, 0), (0, 1), (1, 1))
CHUNKS = 4
ROWS = DV // CHUNKS
MESH = pl.DeviceIdType.MESH


def flip(index):
    return index + RING - 2 * RING * (index // RING)


def prep_kernel(tiles_ref, mask_ref, amp_ref, chol_ref, pack_ref, weighted_ref, sems):
    i = lax.axis_index("orow")
    half = lax.axis_index("ocol") // RING
    copies = []
    for s in range(RING + 1):
        if s < RING:
            j = half * RING + s
            other = jnp.logical_and(i // RING == half, i > j)
            a = jnp.where(other, flip(i), i)
            b = jnp.where(other, flip(j), j)
        else:
            a = b = flip(i)
        picks = (tiles_ref[a, b, 0], tiles_ref[a, b, 1])
        for k, (r, c) in enumerate(PARTS):
            copy = pltpu.make_async_copy(
                chol_ref.at[
                    0,
                    pl.ds(pl.multiple_of(picks[r] * TILE, TILE), TILE),
                    pl.ds(pl.multiple_of(picks[c] * TILE, TILE), TILE),
                ],
                pack_ref.at[s, k],
                sems.at[s * 3 + k],
            )
            copy.start()
            copies.append(copy)
    for s in range(2):
        for t in range(2):
            block = (pl.ds(s * TILE, TILE), pl.ds(t * TILE, TILE))
            keep = mask_ref[0, 0, s, t].astype(jnp.float32).astype(jnp.bfloat16)
            weighted_ref[block] = amp_ref[(0, 0) + block] * keep
    for copy in copies:
        copy.wait()


def ladder_kernel(
    pack_ref, weighted_ref, out_ref,
    slots, extra, factor, inputs, inner, total, give, give_more, got, got_more,
    f_send, f_recv, x_send, x_recv, w_send, w_recv, p_send, p_recv, m_send, m_recv,
):
    i = lax.axis_index("orow")
    j = lax.axis_index("ocol")
    half = j // RING
    me = j - half * RING
    y, core = me // 2, me % 2
    fi, fj = flip(i), flip(j)
    same = i // RING == half
    diag = i == j
    lower = jnp.logical_and(same, i > j)
    upper = jnp.logical_and(same, i < j)
    swapped = jnp.logical_and(same, i <= j)
    dflag = jnp.where(diag, 1, 0)
    w_dev = (jnp.where(swapped, fj, j), jnp.where(swapped, fi, i))
    p_swap = jnp.logical_or(lower, diag)
    p_dev = (jnp.where(p_swap, fj, j), jnp.where(p_swap, fi, i))
    m_dev = (fi, fj)

    def peer(k):
        step = k // 2
        dy = step + step // 2 - 2 * (step // 3)
        return ((y + dy) % 4) * 2 + (core + k) % 2

    barrier = pltpu.get_barrier_semaphore()

    def greet(device):
        pl.semaphore_signal(barrier, inc=1, device_id=device, device_id_type=MESH)

    for k in range(1, RING):
        greet((i, half * RING + peer(k)))
    greet(w_dev)

    @pl.when(jnp.logical_or(upper, lower))
    def _():
        greet(p_dev)

    @pl.when(lower)
    def _():
        greet(m_dev)

    pl.semaphore_wait(barrier, RING + jnp.where(i == j, 0, jnp.where(same, 1, 0)) + jnp.where(lower, 1, 0))

    def remote(src, dst, send, recv, device):
        return pltpu.make_async_remote_copy(
            src_ref=src, dst_ref=dst, send_sem=send, recv_sem=recv, device_id=device, device_id_type=MESH
        )

    w_copy = remote(weighted_ref, inputs.at[1], w_send.at[1], w_recv.at[1], w_dev)
    w_more = remote(weighted_ref, inputs.at[0], w_send.at[0], w_recv.at[0], m_dev)
    w_own = pltpu.make_async_copy(weighted_ref, inputs.at[0], w_recv.at[0])
    w_copy.start()

    @pl.when(lower)
    def _():
        w_more.start()

    @pl.when(jnp.logical_not(lower))
    def _():
        w_own.start()

    def f_copy(k):
        to = peer(k)
        return remote(pack_ref.at[to], slots.at[me], f_send.at[k], f_recv.at[me], (i, half * RING + to))

    f_own = pltpu.make_async_copy(pack_ref.at[me], slots.at[me], f_send.at[0])
    f_own.start()
    x_copy = remote(pack_ref.at[RING], extra.at[me], x_send.at[0], x_recv.at[me], (i, i))
    x_own = pltpu.make_async_copy(pack_ref.at[RING], extra.at[me], x_send.at[1])
    for k in range(1, RING):
        f_copy(k).start()

    @pl.when(jnp.logical_and(same, jnp.logical_not(diag)))
    def _():
        x_copy.start()

    @pl.when(diag)
    def _():
        x_own.start()

    total[...] = jnp.zeros_like(total)
    w_copy.wait_recv()

    @pl.when(lower)
    def _():
        w_more.wait_recv()

    @pl.when(jnp.logical_not(lower))
    def _():
        w_own.wait()

    f_own.wait()

    @pl.when(diag)
    def _():
        x_own.wait()

    def build(source, slot, which):
        factor[which, :TILE, :TILE] = source[slot, 0]
        factor[which, :TILE, TILE:] = source[slot, 1]
        factor[which, TILE:, :TILE] = source[slot, 1].T
        factor[which, TILE:, TILE:] = source[slot, 2]

    def add(side, which):
        for c in range(2):
            cols = pl.ds(c * TILE, TILE)
            inner[:, cols] = jnp.dot(
                factor[which], inputs[side, :, cols], preferred_element_type=jnp.float32
            ).astype(jnp.bfloat16)
        for c in range(2):
            cols = pl.ds(c * TILE, TILE)
            total[side, :, cols] += jnp.dot(
                inner[...], factor[which, :, cols], preferred_element_type=jnp.float32
            )

    def step(k, carry):
        slot = peer(k)

        @pl.when(k > 0)
        def _():
            remote(pack_ref.at[slot], slots.at[slot], f_send.at[slot], f_recv.at[slot], w_dev).wait_recv()

        build(slots, slot, 0)

        @pl.when(diag)
        def _():
            @pl.when(k > 0)
            def _():
                remote(pack_ref.at[RING], extra.at[slot], x_send.at[0], x_recv.at[slot], w_dev).wait_recv()

            build(extra, slot, 1)

        add(0, 0)
        add(1, dflag)
        return carry

    lax.fori_loop(0, RING, step, 0)

    def p_copy(r):
        return remote(give.at[r], got.at[r], p_send.at[r], p_recv.at[r], p_dev)

    def m_copy(r):
        return remote(give_more.at[r], got_more.at[r], m_send.at[r], m_recv.at[r], m_dev)

    for r in range(CHUNKS):
        rows = pl.ds(r * ROWS, ROWS)
        give[r] = (total[1, rows, :] + total[dflag, :, rows].T).astype(jnp.bfloat16)
        p_copy(r).start()
        own = total[0, rows, :] + total[1 - dflag, :, rows].T
        out_ref[rows, :] = own

        @pl.when(lower)
        def _():
            give_more[r] = own.astype(jnp.bfloat16)
            m_copy(r).start()

    for r in range(CHUNKS):
        rows = pl.ds(r * ROWS, ROWS)
        p_copy(r).wait_recv()

        @pl.when(lower)
        def _():
            m_copy(r).wait_recv()
            out_ref[rows, :] = got[r].astype(jnp.float32) + got_more[r].astype(jnp.float32)

        @pl.when(jnp.logical_not(lower))
        def _():
            out_ref[rows, :] += got[r].astype(jnp.float32)

    w_copy.wait_send()
    for k in range(1, RING):
        f_copy(k).wait_send()
    for r in range(CHUNKS):
        p_copy(r).wait_send()

    @pl.when(jnp.logical_and(same, jnp.logical_not(diag)))
    def _():
        x_copy.wait_send()

    @pl.when(lower)
    def _():
        w_more.wait_send()
        for r in range(CHUNKS):
            m_copy(r).wait_send()


def shards(amplitudes, tile_mask, domain_tiles, cholesky):
    vmem = pl.BlockSpec(memory_space=pltpu.VMEM)
    smem = pl.BlockSpec(memory_space=pltpu.SMEM)
    dma = pltpu.SemaphoreType.DMA
    half = jnp.bfloat16
    pack, weighted = pl.pallas_call(
        prep_kernel,
        out_shape=(
            pltpu.VMEM((RING + 1, 3, TILE, TILE), half),
            pltpu.VMEM((DV, DV), half),
        ),
        in_specs=[smem, smem, vmem, pl.BlockSpec(memory_space=pl.ANY)],
        out_specs=(vmem, vmem),
        scratch_shapes=[dma((3 * RING + 3,))],
        compiler_params=pltpu.CompilerParams(vmem_limit_bytes=56 << 20),
        name="prep",
    )(domain_tiles, tile_mask, amplitudes, cholesky)
    ladder = pl.pallas_call(
        ladder_kernel,
        out_shape=jax.ShapeDtypeStruct((DV, DV), jnp.float32),
        in_specs=[vmem, vmem],
        out_specs=vmem,
        scratch_shapes=[
            pltpu.VMEM((RING, 3, TILE, TILE), half),
            pltpu.VMEM((RING, 3, TILE, TILE), half),
            pltpu.VMEM((2, DV, DV), half),
            pltpu.VMEM((2, DV, DV), half),
            pltpu.VMEM((DV, DV), half),
            pltpu.VMEM((2, DV, DV), jnp.float32),
            pltpu.VMEM((CHUNKS, ROWS, DV), half),
            pltpu.VMEM((CHUNKS, ROWS, DV), half),
            pltpu.VMEM((CHUNKS, ROWS, DV), half),
            pltpu.VMEM((CHUNKS, ROWS, DV), half),
            dma((RING,)), dma((RING,)), dma((2,)), dma((RING,)), dma((2,)), dma((2,)),
            dma((CHUNKS,)), dma((CHUNKS,)), dma((CHUNKS,)), dma((CHUNKS,)),
        ],
        compiler_params=pltpu.CompilerParams(
            collective_id=0, has_side_effects=True, vmem_limit_bytes=36 << 20
        ),
        name="ladder",
    )(pack, weighted)
    return ladder.reshape(1, 1, DV, DV)


def solution(mesh):
    return jax.shard_map(
        shards,
        mesh=mesh,
        in_specs=(
            P("orow", "ocol", None, None),
            P("orow", "ocol", None, None),
            P(),
            P("ocol", None, None),
        ),
        out_specs=P("orow", "ocol", None, None),
        check_vma=False,
    )
```

time: 468 us -> 112 us (0.24)
  the two profiles are of different devices: /device:TPU:5 before, /device:TPU:37 now
where the time goes in v1:
time: 112 us
  Pallas kernels  110 us (98%)
  local copies, waits for them, and re-layouts  2.51 us (2%)
    pallas_call x1, Pallas kernels, shards(): pl.pallas_call(ladder_kernel, out_shape=jax.ShapeDtypeStruct((DV, DV), jn...  104 us
    pallas_call x1, Pallas kernels, shards(): pl.pallas_call(prep_kernel, out_shape=(pltpu.VMEM((RING + 1, 3, TILE, TIL...  5.22 us
    unnamed x2, local copies, waits for them, and re-layouts  2.51 us

profile of v1, /device:TPU:37, one launch (start us, length us, event | category | flops | bytes accessed | tf_op | source)
XLA Modules:
  0.0 112.0 jit_solution(1393366884500932079)
XLA Ops:
  0.0 1.5 %copy.5.tiles_ref = s32[16,16,2]{2,1,0:T(8,128)} copy(s32[16,16,2]{1,2,0:T(2,128)} %param.6) | data formatting | bytes 4096 | tf_op args[2]
  1.5 5.2 %prep.1 = (bf16[9,3,256,256]{3,2,1,0:T(8,128)(2,1)S(1)}, bf16[512,512]{1,0:T(8,128)(2,1)S(1)}) custom-call(s32[16,16,2]{2,1,0:T(8,128)} %copy.5.tiles_ref, s32[1,1,2,2]{3,2,1,0:T(2,128)} %mask_ref.1, bf16[1,1,512,512]{3,2,1,0:T(8,128)(2,1)} %amp_ref.1, bf16[1,2048,2048]{2,1,0:T(8,128)(2,1)} %chol_ref.1), custom_call_target="tpu_custom_call" | custom-call | tf_op jit(solution)/shard_map/prep/pallas_call | solution.py:252
  6.8 104.3 %ladder.1 = f32[512,512]{1,0:T(8,128)S(1)} custom-call(bf16[9,3,256,256]{3,2,1,0:T(8,128)(2,1)S(1)} %get-tuple-element.7.pack_ref, bf16[512,512]{1,0:T(8,128)(2,1)S(1)} %get-tuple-element.8.weighted_ref), custom_call_target="tpu_custom_call" | custom-call | tf_op jit(solution)/shard_map/ladder/pallas_call | solution.py:264
  111.1 1.0 copy.7

commit v2 on v1

v2 whole, which is shorter than its diff:
```python
import jax
import jax.numpy as jnp
from jax import lax
from jax.experimental import pallas as pl
from jax.experimental.pallas import tpu as pltpu
from jax.sharding import PartitionSpec as P

TILE = 256
HT = 128
DV = 512
NO = 16
RING = 8
CHUNKS = 4
ROWS = DV // CHUNKS
PACK = 8 * HT + 16
MESH = pl.DeviceIdType.MESH


def flip(index):
    return index + RING - 2 * RING * (index // RING)


def corner(shape=(HT, HT)):
    return lax.broadcasted_iota(jnp.int32, shape, 0), lax.broadcasted_iota(jnp.int32, shape, 1)


def prep_kernel(tiles_ref, mask_ref, amp_ref, chol_ref, pack_ref, weighted_ref, stage, raw, sems, raw_sem):
    i = lax.axis_index("orow")
    half = lax.axis_index("ocol") // RING
    raw_copy = pltpu.make_async_copy(amp_ref, raw, raw_sem)
    copies = []
    for s in range(RING + 1):
        if s < RING:
            j = half * RING + s
            other = jnp.logical_and(i // RING == half, i > j)
            a = jnp.where(other, flip(i), i)
            b = jnp.where(other, flip(j), j)
        else:
            a = b = flip(i)
        t0 = tiles_ref[a, 0, b] * TILE
        t1 = tiles_ref[a, 1, b] * TILE

        def pick(row, col, height, dst, sem):
            copy = pltpu.make_async_copy(
                chol_ref.at[0, pl.ds(pl.multiple_of(row, HT), height), pl.ds(pl.multiple_of(col, HT), HT)], dst, sem
            )
            copy.start()
            return copy

        mine = []
        for n, (t, off) in enumerate(((t0, 0), (t0, HT), (t1, 0), (t1, HT))):
            mine.append(pick(t + off, t + off, HT, stage.at[s, n], sems.at[s, n]))
        for n, (row, col, height, at) in enumerate(
            ((t0, t1, TILE, 0), (t0, t1 + HT, TILE, TILE), (t0, t0 + HT, HT, 2 * TILE), (t1, t1 + HT, HT, 2 * TILE + HT))
        ):
            mine.append(pick(row, col, height, pack_ref.at[s, pl.ds(at, height)], sems.at[s, 4 + n]))
        copies.append(mine)
        if s == 0:
            raw_copy.start()
    row, col = corner()
    line = lax.broadcasted_iota(jnp.int32, (16, HT), 0)
    raw_copy.wait()
    for s in range(2):
        for t in range(2):
            keep = mask_ref[0, 0, s, t].astype(jnp.float32).astype(jnp.bfloat16)
            weighted_ref[t, pl.ds(s * TILE, TILE), :] = raw[0, 0, pl.ds(s * TILE, TILE), pl.ds(t * TILE, TILE)] * keep
    for s in range(RING + 1):
        for n in range(4):
            copies[s][n].wait()
        blocks = [stage[s, n].astype(jnp.float32) for n in range(4)]
        pack_ref[s, 6 * HT : 7 * HT, :] = jnp.where(row <= col, blocks[0], blocks[1]).astype(jnp.bfloat16)
        pack_ref[s, 7 * HT : 8 * HT, :] = jnp.where(row <= col, blocks[2], blocks[3]).astype(jnp.bfloat16)
        ends = [jnp.sum(jnp.where(row == col, blocks[n], 0.0), axis=0, keepdims=True) for n in (1, 3)]
        pack_ref[s, 8 * HT :, :] = jnp.where(line == 0, ends[0], ends[1]).astype(jnp.bfloat16)
    for s in range(RING + 1):
        for n in range(4, 8):
            copies[s][n].wait()


def ladder_kernel(
    pack_ref, weighted_ref, out_ref,
    slots, extra, factor, inputs, inner, total, give, got, pass_on, passed,
    f_send, f_recv, x_send, x_recv, w_send, w_recv, p_send, p_recv, m_send, m_recv,
):
    i = lax.axis_index("orow")
    j = lax.axis_index("ocol")
    half = j // RING
    me = j - half * RING
    y, core = me // 2, me % 2
    fi, fj = flip(i), flip(j)
    same = i // RING == half
    diag = i == j
    lower = jnp.logical_and(same, i > j)
    upper = jnp.logical_and(same, i < j)
    not_lower = jnp.logical_not(lower)
    not_upper = jnp.logical_not(upper)
    swapped = jnp.logical_and(same, i <= j)
    dflag = jnp.where(diag, 1, 0)
    w_dev = (jnp.where(swapped, fj, j), jnp.where(swapped, fi, i))
    p_swap = jnp.logical_or(lower, diag)
    p_dev = (jnp.where(p_swap, fj, j), jnp.where(p_swap, fi, i))
    m_dev = (fi, fj)
    t_dev = (j, i)

    def peer(k):
        step = k // 2
        dy = step + step // 2 - 2 * (step // 3)
        return ((y + dy) % 4) * 2 + (core + k) % 2

    barrier = pltpu.get_barrier_semaphore()

    def greet(device):
        pl.semaphore_signal(barrier, inc=1, device_id=device, device_id_type=MESH)

    for k in range(1, RING):
        greet((i, half * RING + peer(k)))
    greet(w_dev)

    @pl.when(jnp.logical_or(upper, lower))
    def _():
        greet(p_dev)

    @pl.when(lower)
    def _():
        greet(m_dev)

    pl.semaphore_wait(barrier, RING + jnp.where(diag, 0, jnp.where(same, 1, 0)) + jnp.where(lower, 1, 0))

    def remote(src, dst, send, recv, device):
        return pltpu.make_async_remote_copy(
            src_ref=src, dst_ref=dst, send_sem=send, recv_sem=recv, device_id=device, device_id_type=MESH
        )

    def w_copy(h):
        return remote(weighted_ref.at[h], inputs.at[1, h], w_send.at[1, h], w_recv.at[1, h], w_dev)

    def w_more(h):
        return remote(weighted_ref.at[h], inputs.at[0, h], w_send.at[0, h], w_recv.at[0, h], m_dev)

    def w_own(h):
        return pltpu.make_async_copy(weighted_ref.at[h], inputs.at[0, h], w_recv.at[0, h])

    for h in range(2):
        w_copy(h).start()

        @pl.when(lower)
        def _():
            w_more(h).start()

        @pl.when(not_lower)
        def _():
            w_own(h).start()

    def f_copy(k):
        to = peer(k)
        return remote(pack_ref.at[to], slots.at[me], f_send.at[k], f_recv.at[me], (i, half * RING + to))

    f_own = pltpu.make_async_copy(pack_ref.at[me], slots.at[me], f_send.at[0])
    f_own.start()
    x_copy = remote(pack_ref.at[RING], extra.at[me], x_send.at[0], x_recv.at[me], (i, i))
    x_own = pltpu.make_async_copy(pack_ref.at[RING], extra.at[me], x_send.at[1])
    for k in range(1, RING):
        f_copy(k).start()

    @pl.when(jnp.logical_and(same, jnp.logical_not(diag)))
    def _():
        x_copy.start()

    @pl.when(diag)
    def _():
        x_own.start()

    total[...] = jnp.zeros_like(total)

    @pl.when(not_lower)
    def _():
        for h in range(2):
            w_own(h).wait()

    f_own.wait()

    @pl.when(diag)
    def _():
        x_own.wait()

    row, col = corner()

    def build(source, slot, which):
        for n in range(2):
            at = n * TILE
            side = source[slot, 4 * HT + n * HT : 5 * HT + n * HT, :]
            mixed = source[slot, 6 * HT + n * HT : 7 * HT + n * HT, :].astype(jnp.float32)
            turned = mixed.T
            ends = source[slot, 8 * HT :, :].astype(jnp.float32)[n : n + 1, :]
            factor[which, at : at + HT, at : at + HT] = jnp.where(row <= col, mixed, turned).astype(jnp.bfloat16)
            factor[which, at : at + HT, at + HT : at + TILE] = side
            factor[which, at + HT : at + TILE, at : at + HT] = side.T
            factor[which, at + HT : at + TILE, at + HT : at + TILE] = jnp.where(
                row > col, mixed, jnp.where(row == col, ends, turned)
            ).astype(jnp.bfloat16)
            block = source[slot, n * TILE : n * TILE + TILE, :]
            factor[which, :TILE, TILE + n * HT : TILE + n * HT + HT] = block
            factor[which, TILE + n * HT : TILE + n * HT + HT, :TILE] = block.T

    def add(side, h, which):
        inner[...] = jnp.dot(factor[which], inputs[side, h], preferred_element_type=jnp.float32).astype(jnp.bfloat16)
        for c in range(2):
            cols = pl.ds(c * TILE, TILE)
            total[side, :, cols] += jnp.dot(
                inner[...], factor[which, h * TILE : h * TILE + TILE, cols], preferred_element_type=jnp.float32
            )

    def add_remote(h, slot):
        add(1, h, slot + RING * dflag)

        @pl.when(lower)
        def _():
            add(0, h, slot)

    def await_inputs(h):
        w_copy(h).wait_recv()

        @pl.when(lower)
        def _():
            w_more(h).wait_recv()

    def arrive(k):
        slot = peer(k)

        @pl.when(k > 0)
        def _():
            remote(pack_ref.at[slot], slots.at[slot], f_send.at[slot], f_recv.at[slot], w_dev).wait_recv()

        build(slots, slot, slot)

        @pl.when(diag)
        def _():
            @pl.when(k > 0)
            def _():
                remote(pack_ref.at[RING], extra.at[slot], x_send.at[0], x_recv.at[slot], w_dev).wait_recv()

            build(extra, slot, slot + RING)

        @pl.when(not_lower)
        def _():
            add(0, 0, slot)
            add(0, 1, slot)

    def first(k, carry):
        arrive(k)

        @pl.when(k == RING // 2)
        def _():
            await_inputs(0)

        @pl.when(k >= RING // 2)
        def _():
            def again(n, carry):
                add_remote(0, peer(k - n * (RING // 2)))
                return carry

            lax.fori_loop(0, 2, again, 0)

        return carry

    lax.fori_loop(0, RING, first, 0)
    await_inputs(1)

    def second(k, carry):
        add_remote(1, k)
        return carry

    lax.fori_loop(0, RING, second, 0)

    def p_copy(r):
        return remote(give.at[r], got.at[r], p_send.at[r], p_recv.at[r], p_dev)

    def m_copy(r):
        return remote(pass_on.at[r], passed.at[r], m_send.at[r], m_recv.at[r], t_dev)

    @pl.when(not_upper)
    def _():
        for r in range(CHUNKS):
            rows = pl.ds(r * ROWS, ROWS)
            give[r] = (total[1, rows, :] + total[dflag, :, rows].T).astype(jnp.bfloat16)
            p_copy(r).start()

    @pl.when(not_lower)
    def _():
        for r in range(CHUNKS):
            rows = pl.ds(r * ROWS, ROWS)
            out_ref[rows, :] = total[0, rows, :] + total[1 - dflag, :, rows].T
        for r in range(CHUNKS):
            rows = pl.ds(r * ROWS, ROWS)
            p_copy(r).wait_recv()
            ours = out_ref[rows, :] + got[r].astype(jnp.float32)
            out_ref[rows, :] = ours

            @pl.when(upper)
            def _():
                pass_on[r] = ours.astype(jnp.bfloat16)
                m_copy(r).start()

    @pl.when(lower)
    def _():
        for r in range(CHUNKS):
            m_copy(r).wait_recv()
            out_ref[:, pl.ds(r * ROWS, ROWS)] = passed[r].astype(jnp.float32).T

    for h in range(2):
        w_copy(h).wait_send()
    for k in range(1, RING):
        f_copy(k).wait_send()

    @pl.when(not_upper)
    def _():
        for r in range(CHUNKS):
            p_copy(r).wait_send()

    @pl.when(upper)
    def _():
        for r in range(CHUNKS):
            m_copy(r).wait_send()

    @pl.when(jnp.logical_and(same, jnp.logical_not(diag)))
    def _():
        x_copy.wait_send()

    @pl.when(lower)
    def _():
        for h in range(2):
            w_more(h).wait_send()


def shards(amplitudes, tile_mask, domain_tiles, cholesky):
    vmem = pl.BlockSpec(memory_space=pltpu.VMEM)
    smem = pl.BlockSpec(memory_space=pltpu.SMEM)
    hbm = pl.BlockSpec(memory_space=pl.ANY)
    dma = pltpu.SemaphoreType.DMA
    half = jnp.bfloat16
    pack, weighted = pl.pallas_call(
        prep_kernel,
        out_shape=(
            pltpu.VMEM((RING + 1, PACK, HT), half),
            pltpu.VMEM((2, DV, TILE), half),
        ),
        in_specs=[smem, smem, hbm, hbm],
        out_specs=(vmem, vmem),
        scratch_shapes=[
            pltpu.VMEM((RING + 1, 4, HT, HT), half),
            pltpu.VMEM((1, 1, DV, DV), half),
            dma((RING + 1, 8)),
            dma,
        ],
        compiler_params=pltpu.CompilerParams(vmem_limit_bytes=56 << 20),
        name="prep",
    )(domain_tiles.transpose(0, 2, 1), tile_mask, amplitudes, cholesky)
    ladder = pl.pallas_call(
        ladder_kernel,
        out_shape=jax.ShapeDtypeStruct((DV, DV), jnp.float32),
        in_specs=[vmem, vmem],
        out_specs=vmem,
        scratch_shapes=[
            pltpu.VMEM((RING, PACK, HT), half),
            pltpu.VMEM((RING, PACK, HT), half),
            pltpu.VMEM((2 * RING, DV, DV), half),
            pltpu.VMEM((2, 2, DV, TILE), half),
            pltpu.VMEM((DV, TILE), half),
            pltpu.VMEM((2, DV, DV), jnp.float32),
            pltpu.VMEM((CHUNKS, ROWS, DV), half),
            pltpu.VMEM((CHUNKS, ROWS, DV), half),
            pltpu.VMEM((CHUNKS, ROWS, DV), half),
            pltpu.VMEM((CHUNKS, ROWS, DV), half),
            dma((RING,)), dma((RING,)), dma((2,)), dma((RING,)), dma((2, 2)), dma((2, 2)),
            dma((CHUNKS,)), dma((CHUNKS,)), dma((CHUNKS,)), dma((CHUNKS,)),
        ],
        compiler_params=pltpu.CompilerParams(
            collective_id=0, has_side_effects=True, vmem_limit_bytes=36 << 20
        ),
        name="ladder",
    )(pack, weighted)
    return ladder.reshape(1, 1, DV, DV)


def solution(mesh):
    return jax.shard_map(
        shards,
        mesh=mesh,
        in_specs=(
            P("orow", "ocol", None, None),
            P("orow", "ocol", None, None),
            P(),
            P("ocol", None, None),
        ),
        out_specs=P("orow", "ocol", None, None),
        check_vma=False,
    )
```

time: 112 us -> 107 us (0.955)
  the two profiles are of different devices: /device:TPU:37 before, /device:TPU:36 now
where the time goes in v2:
time: 107 us
  Pallas kernels  106 us (99%)
    pallas_call x1, Pallas kernels, shards(): pl.pallas_call(ladder_kernel, out_shape=jax.ShapeDtypeStruct((DV, DV), jn...  102 us
    pallas_call x1, Pallas kernels, shards(): pl.pallas_call(prep_kernel, out_shape=(pltpu.VMEM((RING + 1, PACK, HT), h...  4.35 us

profile of v2, /device:TPU:36, one launch (start us, length us, event | category | flops | bytes accessed | tf_op | source)
XLA Modules:
  0.0 107.2 jit_solution(16968319161927298496)
XLA Ops:
  0.0 4.4 %prep.1 = (bf16[9,1040,128]{2,1,0:T(8,128)(2,1)S(1)}, bf16[2,512,256]{2,1,0:T(8,128)(2,1)S(1)}) custom-call(s32[16,2,16]{2,1,0:T(2,128)} %bitcast.3, s32[1,1,2,2]{3,2,1,0:T(2,128)} %mask_ref.1, bf16[1,1,512,512]{3,2,1,0:T(8,128)(2,1)} %amp_ref.1, bf16[1,2048,2048]{2,1,0:T(8,128)(2,1)} %chol_ref.1), custom_call_target="tpu_custom_call" | custom-call | tf_op jit(solution)/shard_map/prep/pallas_call | solution.py:341
  4.4 101.8 %ladder.1 = f32[512,512]{1,0:T(8,128)S(1)} custom-call(bf16[9,1040,128]{2,1,0:T(8,128)(2,1)S(1)} %get-tuple-element.7.pack_ref, bf16[2,512,256]{2,1,0:T(8,128)(2,1)S(1)} %get-tuple-element.8.weighted_ref), custom_call_target="tpu_custom_call" | custom-call | tf_op jit(solution)/shard_map/ladder/pallas_call | solution.py:358
  106.2 1.0 copy.6

commit v3 on v2

--- a/solution.py
+++ b/solution.py
@@ -11,13 +11,21 @@
 NO = 16
 RING = 8
 CHUNKS = 4
+SENDS = 8
+LATE = 5
 ROWS = DV // CHUNKS
+PART = DV // SENDS
 PACK = 8 * HT + 16
 MESH = pl.DeviceIdType.MESH
 
 
 def flip(index):
     return index + RING - 2 * RING * (index // RING)
+
+
+def gives(i, j):
+    even = (i // 4 + j // 4 + i + j) % 2 == 0
+    return jnp.logical_or(jnp.logical_and(i > j, jnp.logical_not(even)), jnp.logical_and(i < j, even))
 
 
 def corner(shape=(HT, HT)):
@@ -32,7 +40,7 @@
     for s in range(RING + 1):
         if s < RING:
             j = half * RING + s
-            other = jnp.logical_and(i // RING == half, i > j)
+            other = jnp.logical_and(i // RING == half, gives(i, j))
             a = jnp.where(other, flip(i), i)
             b = jnp.where(other, flip(j), j)
         else:
@@ -90,11 +98,11 @@
     fi, fj = flip(i), flip(j)
     same = i // RING == half
     diag = i == j
-    lower = jnp.logical_and(same, i > j)
-    upper = jnp.logical_and(same, i < j)
+    lower = jnp.logical_and(same, gives(i, j))
+    upper = jnp.logical_and(same, gives(j, i))
     not_lower = jnp.logical_not(lower)
     not_upper = jnp.logical_not(upper)
-    swapped = jnp.logical_and(same, i <= j)
+    swapped = jnp.logical_or(upper, diag)
     dflag = jnp.where(diag, 1, 0)
     w_dev = (jnp.where(swapped, fj, j), jnp.where(swapped, fi, i))
     p_swap = jnp.logical_or(lower, diag)
@@ -202,36 +210,34 @@
             factor[which, :TILE, TILE + n * HT : TILE + n * HT + HT] = block
             factor[which, TILE + n * HT : TILE + n * HT + HT, :TILE] = block.T
 
-    def add(side, h, which):
-        inner[...] = jnp.dot(factor[which], inputs[side, h], preferred_element_type=jnp.float32).astype(jnp.bfloat16)
+    def add(side, which):
+        for h in range(2):
+            inner[:, h * TILE : h * TILE + TILE] = jnp.dot(
+                factor[which], inputs[side, h], preferred_element_type=jnp.float32
+            ).astype(jnp.bfloat16)
         for c in range(2):
             cols = pl.ds(c * TILE, TILE)
             total[side, :, cols] += jnp.dot(
-                inner[...], factor[which, h * TILE : h * TILE + TILE, cols], preferred_element_type=jnp.float32
+                inner[...], factor[which, :, cols], preferred_element_type=jnp.float32
             )
 
-    def add_remote(h, slot):
-        add(1, h, slot + RING * dflag)
+    def await_inputs():
+        for h in range(2):
+            w_copy(h).wait_recv()
 
         @pl.when(lower)
         def _():
-            add(0, h, slot)
-
-    def await_inputs(h):
-        w_copy(h).wait_recv()
-
-        @pl.when(lower)
-        def _():
-            w_more(h).wait_recv()
-
-    def arrive(k):
+            for h in range(2):
+                w_more(h).wait_recv()
+
+    def step(k, carry):
         slot = peer(k)
 
         @pl.when(k > 0)
         def _():
             remote(pack_ref.at[slot], slots.at[slot], f_send.at[slot], f_recv.at[slot], w_dev).wait_recv()
 
-        build(slots, slot, slot)
+        build(slots, slot, k)
 
         @pl.when(diag)
         def _():
@@ -239,38 +245,29 @@
             def _():
                 remote(pack_ref.at[RING], extra.at[slot], x_send.at[0], x_recv.at[slot], w_dev).wait_recv()
 
-            build(extra, slot, slot + RING)
+            build(extra, slot, k + RING)
 
         @pl.when(not_lower)
         def _():
-            add(0, 0, slot)
-            add(0, 1, slot)
-
-    def first(k, carry):
-        arrive(k)
-
-        @pl.when(k == RING // 2)
-        def _():
-            await_inputs(0)
-
-        @pl.when(k >= RING // 2)
-        def _():
-            def again(n, carry):
-                add_remote(0, peer(k - n * (RING // 2)))
-                return carry
-
-            lax.fori_loop(0, 2, again, 0)
-
+            add(0, k)
+
+        @pl.when(k == LATE)
+        def _():
+            await_inputs()
+
+        def again(n, carry):
+            add(1, n + RING * dflag)
+
+            @pl.when(lower)
+            def _():
+                add(0, n)
+
+            return carry
+
+        lax.fori_loop(jnp.where(k == LATE, 0, k), jnp.where(k < LATE, 0, k + 1), again, 0)
         return carry
 
-    lax.fori_loop(0, RING, first, 0)
-    await_inputs(1)
-
-    def second(k, carry):
-        add_remote(1, k)
-        return carry
-
-    lax.fori_loop(0, RING, second, 0)
+    lax.fori_loop(0, RING, step, 0)
 
     def p_copy(r):
         return remote(give.at[r], got.at[r], p_send.at[r], p_recv.at[r], p_dev)
@@ -282,16 +279,18 @@
     def _():
         for r in range(CHUNKS):
             rows = pl.ds(r * ROWS, ROWS)
-            give[r] = (total[1, rows, :] + total[dflag, :, rows].T).astype(jnp.bfloat16)
-            p_copy(r).start()
+            ours = (total[1, rows, :] + total[dflag, :, rows].T).astype(jnp.bfloat16)
+            for n in range(2):
+                give[2 * r + n] = ours[n * PART : (n + 1) * PART]
+                p_copy(2 * r + n).start()
 
     @pl.when(not_lower)
     def _():
         for r in range(CHUNKS):
             rows = pl.ds(r * ROWS, ROWS)
             out_ref[rows, :] = total[0, rows, :] + total[1 - dflag, :, rows].T
-        for r in range(CHUNKS):
-            rows = pl.ds(r * ROWS, ROWS)
+        for r in range(SENDS):
+            rows = pl.ds(r * PART, PART)
             p_copy(r).wait_recv()
             ours = out_ref[rows, :] + got[r].astype(jnp.float32)
             out_ref[rows, :] = ours
@@ -304,8 +303,10 @@
     @pl.when(lower)
     def _():
         for r in range(CHUNKS):
-            m_copy(r).wait_recv()
-            out_ref[:, pl.ds(r * ROWS, ROWS)] = passed[r].astype(jnp.float32).T
+            for n in range(2):
+                m_copy(2 * r + n).wait_recv()
+            both = jnp.concatenate([passed[2 * r], passed[2 * r + 1]], axis=0)
+            out_ref[:, pl.ds(r * ROWS, ROWS)] = both.astype(jnp.float32).T
 
     for h in range(2):
         w_copy(h).wait_send()
@@ -314,12 +315,12 @@
 
     @pl.when(not_upper)
     def _():
-        for r in range(CHUNKS):
+        for r in range(SENDS):
             p_copy(r).wait_send()
 
     @pl.when(upper)
     def _():
-        for r in range(CHUNKS):
+        for r in range(SENDS):
             m_copy(r).wait_send()
 
     @pl.when(jnp.logical_and(same, jnp.logical_not(diag)))
@@ -365,14 +366,14 @@
             pltpu.VMEM((RING, PACK, HT), half),
             pltpu.VMEM((2 * RING, DV, DV), half),
             pltpu.VMEM((2, 2, DV, TILE), half),
-            pltpu.VMEM((DV, TILE), half),
+            pltpu.VMEM((DV, DV), half),
             pltpu.VMEM((2, DV, DV), jnp.float32),
-            pltpu.VMEM((CHUNKS, ROWS, DV), half),
-            pltpu.VMEM((CHUNKS, ROWS, DV), half),
-            pltpu.VMEM((CHUNKS, ROWS, DV), half),
-            pltpu.VMEM((CHUNKS, ROWS, DV), half),
+            pltpu.VMEM((SENDS, PART, DV), half),
+            pltpu.VMEM((SENDS, PART, DV), half),
+            pltpu.VMEM((SENDS, PART, DV), half),
+            pltpu.VMEM((SENDS, PART, DV), half),
             dma((RING,)), dma((RING,)), dma((2,)), dma((RING,)), dma((2, 2)), dma((2, 2)),
-            dma((CHUNKS,)), dma((CHUNKS,)), dma((CHUNKS,)), dma((CHUNKS,)),
+            dma((SENDS,)), dma((SENDS,)), dma((SENDS,)), dma((SENDS,)),
         ],
         compiler_params=pltpu.CompilerParams(
             collective_id=0, has_side_effects=True, vmem_limit_bytes=36 << 20

time: 107 us -> 96.4 us (0.901)
  the two profiles are of different devices: /device:TPU:36 before, /device:TPU:156 now
where the time goes in v3:
time: 96.4 us; the launch traced here: 96.3 us
  Pallas kernels  95.3 us (99%)
  local copies, waits for them, and re-layouts  0.97 us (1%)
    pallas_call x1, Pallas kernels, shards(): pl.pallas_call(ladder_kernel, out_shape=jax.ShapeDtypeStruct((DV, DV), jn...  90.9 us
    pallas_call x1, Pallas kernels, shards(): pl.pallas_call(prep_kernel, out_shape=(pltpu.VMEM((RING + 1, PACK, HT), h...  4.38 us

profile of v3, /device:TPU:156, one launch (start us, length us, event | category | flops | bytes accessed | tf_op | source)
XLA Modules:
  0.0 96.3 jit_solution(4961682057203575639)
XLA Ops:
  0.0 4.4 %prep.1 = (bf16[9,1040,128]{2,1,0:T(8,128)(2,1)S(1)}, bf16[2,512,256]{2,1,0:T(8,128)(2,1)S(1)}) custom-call(s32[16,2,16]{2,1,0:T(2,128)} %bitcast.3, s32[1,1,2,2]{3,2,1,0:T(2,128)} %mask_ref.1, bf16[1,1,512,512]{3,2,1,0:T(8,128)(2,1)} %amp_ref.1, bf16[1,2048,2048]{2,1,0:T(8,128)(2,1)} %chol_ref.1), custom_call_target="tpu_custom_call" | custom-call | tf_op jit(solution)/shard_map/prep/pallas_call | solution.py:342
  4.4 90.9 %ladder.1 = f32[512,512]{1,0:T(8,128)S(1)} custom-call(bf16[9,1040,128]{2,1,0:T(8,128)(2,1)S(1)} %get-tuple-element.7.pack_ref, bf16[2,512,256]{2,1,0:T(8,128)(2,1)S(1)} %get-tuple-element.8.weighted_ref), custom_call_target="tpu_custom_call" | custom-call | tf_op jit(solution)/shard_map/ladder/pallas_call | solution.py:359
  95.3 1.0 %copy.6 = f32[1,1,512,512]{3,2,1,0:T(8,128)} copy(f32[1,1,512,512]{3,2,1,0:T(8,128)S(1)} %bitcast.2) | data formatting | bytes 2097152

commit v4 on v3

--- a/solution.py
+++ b/solution.py
@@ -87,8 +87,8 @@
 
 def ladder_kernel(
     pack_ref, weighted_ref, out_ref,
-    slots, extra, factor, inputs, inner, total, give, got, pass_on, passed,
-    f_send, f_recv, x_send, x_recv, w_send, w_recv, p_send, p_recv, m_send, m_recv,
+    slots, extra, through, factor, inputs, inner, total, give, got, pass_on, passed,
+    f_send, f_recv, x_send, x_recv, r_send, r_recv, w_send, w_recv, p_send, p_recv, m_send, m_recv,
 ):
     i = lax.axis_index("orow")
     j = lax.axis_index("ocol")
@@ -115,6 +115,14 @@
         dy = step + step // 2 - 2 * (step // 3)
         return ((y + dy) % 4) * 2 + (core + k) % 2
 
+    entry = (i // 2) % 4
+    ahead = entry % 2 == 0
+    place = (y - entry + 4) % 4
+    detours = jnp.logical_or(place == 0, place == jnp.where(ahead, 1, 3))
+    relays = jnp.logical_not(detours)
+    via = (y + jnp.where(jnp.logical_xor(place == 0, ahead), 1, 3)) % 4
+    origin = (y + jnp.where(jnp.logical_xor(place == 2, ahead), 1, 3)) % 4
+
     barrier = pltpu.get_barrier_semaphore()
 
     def greet(device):
@@ -163,12 +171,33 @@
         to = peer(k)
         return remote(pack_ref.at[to], slots.at[me], f_send.at[k], f_recv.at[me], (i, half * RING + to))
 
+    def detour(n):
+        to = peer(RING - 2 + n)
+        return remote(
+            pack_ref.at[to], through.at[n], f_send.at[RING - 2 + n], r_recv.at[n], (i, half * RING + via * 2 + core)
+        )
+
+    def forward(n):
+        at = origin * 2 + core
+        to = half * RING + (origin + 2) % 4 * 2 + (core + n) % 2
+        return remote(through.at[n], slots.at[at], r_send.at[n], f_recv.at[at], (i, to))
+
     f_own = pltpu.make_async_copy(pack_ref.at[me], slots.at[me], f_send.at[0])
     f_own.start()
     x_copy = remote(pack_ref.at[RING], extra.at[me], x_send.at[0], x_recv.at[me], (i, i))
     x_own = pltpu.make_async_copy(pack_ref.at[RING], extra.at[me], x_send.at[1])
-    for k in range(1, RING):
+    @pl.when(detours)
+    def _():
+        for n in range(2):
+            detour(n).start()
+
+    for k in range(1, RING - 2):
         f_copy(k).start()
+
+    @pl.when(relays)
+    def _():
+        for k in range(RING - 2, RING):
+            f_copy(k).start()
 
     @pl.when(jnp.logical_and(same, jnp.logical_not(diag)))
     def _():
@@ -230,8 +259,28 @@
             for h in range(2):
                 w_more(h).wait_recv()
 
+    def again(n, carry):
+        add(1, n + RING * dflag)
+
+        @pl.when(lower)
+        def _():
+            add(0, n)
+
+        return carry
+
     def step(k, carry):
         slot = peer(k)
+
+        @pl.when(k == LATE)
+        def _():
+            await_inputs()
+            lax.fori_loop(0, LATE, again, 0)
+
+        @pl.when(jnp.logical_and(relays, k == 1))
+        def _():
+            for n in range(2):
+                detour(n).wait_recv()
+                forward(n).start()
 
         @pl.when(k > 0)
         def _():
@@ -251,20 +300,7 @@
         def _():
             add(0, k)
 
-        @pl.when(k == LATE)
-        def _():
-            await_inputs()
-
-        def again(n, carry):
-            add(1, n + RING * dflag)
-
-            @pl.when(lower)
-            def _():
-                add(0, n)
-
-            return carry
-
-        lax.fori_loop(jnp.where(k == LATE, 0, k), jnp.where(k < LATE, 0, k + 1), again, 0)
+        lax.fori_loop(k, jnp.where(k < LATE, k, k + 1), again, 0)
         return carry
 
     lax.fori_loop(0, RING, step, 0)
@@ -312,6 +348,11 @@
         w_copy(h).wait_send()
     for k in range(1, RING):
         f_copy(k).wait_send()
+
+    @pl.when(relays)
+    def _():
+        for n in range(2):
+            forward(n).wait_send()
 
     @pl.when(not_upper)
     def _():
@@ -364,6 +405,7 @@
         scratch_shapes=[
             pltpu.VMEM((RING, PACK, HT), half),
             pltpu.VMEM((RING, PACK, HT), half),
+            pltpu.VMEM((2, PACK, HT), half),
             pltpu.VMEM((2 * RING, DV, DV), half),
             pltpu.VMEM((2, 2, DV, TILE), half),
             pltpu.VMEM((DV, DV), half),
@@ -372,7 +414,7 @@
             pltpu.VMEM((SENDS, PART, DV), half),
             pltpu.VMEM((SENDS, PART, DV), half),
             pltpu.VMEM((SENDS, PART, DV), half),
-            dma((RING,)), dma((RING,)), dma((2,)), dma((RING,)), dma((2, 2)), dma((2, 2)),
+            dma((RING,)), dma((RING,)), dma((2,)), dma((RING,)), dma((2,)), dma((2,)), dma((2, 2)), dma((2, 2)),
             dma((SENDS,)), dma((SENDS,)), dma((SENDS,)), dma((SENDS,)),
         ],
         compiler_params=pltpu.CompilerParams(

time: 96.4 us -> 87.4 us (0.907)
  the two profiles are of different devices: /device:TPU:156 before, /device:TPU:5 now
where the time goes in v4:
time: 87.4 us; the launch traced here: 87.3 us
  Pallas kernels  86.3 us (99%)
  local copies, waits for them, and re-layouts  0.97 us (1%)
    pallas_call x1, Pallas kernels, shards(): pl.pallas_call(ladder_kernel, out_shape=jax.ShapeDtypeStruct((DV, DV), jn...  81.9 us
    pallas_call x1, Pallas kernels, shards(): pl.pallas_call(prep_kernel, out_shape=(pltpu.VMEM((RING + 1, PACK, HT), h...  4.38 us

profile of v4, /device:TPU:5, one launch (start us, length us, event | category | flops | bytes accessed | tf_op | source)
XLA Modules:
  0.0 87.3 jit_solution(9769902810140642961)
XLA Ops:
  0.0 4.4 %prep.1 = (bf16[9,1040,128]{2,1,0:T(8,128)(2,1)S(1)}, bf16[2,512,256]{2,1,0:T(8,128)(2,1)S(1)}) custom-call(s32[16,2,16]{2,1,0:T(2,128)} %bitcast.3, s32[1,1,2,2]{3,2,1,0:T(2,128)} %mask_ref.1, bf16[1,1,512,512]{3,2,1,0:T(8,128)(2,1)} %amp_ref.1, bf16[1,2048,2048]{2,1,0:T(8,128)(2,1)} %chol_ref.1), custom_call_target="tpu_custom_call" | custom-call | tf_op jit(solution)/shard_map/prep/pallas_call | solution.py:383
  4.4 81.9 %ladder.1 = f32[512,512]{1,0:T(8,128)S(1)} custom-call(bf16[9,1040,128]{2,1,0:T(8,128)(2,1)S(1)} %get-tuple-element.7.pack_ref, bf16[2,512,256]{2,1,0:T(8,128)(2,1)S(1)} %get-tuple-element.8.weighted_ref), custom_call_target="tpu_custom_call" | custom-call | tf_op jit(solution)/shard_map/ladder/pallas_call | solution.py:400
  86.3 1.0 %copy.6 = f32[1,1,512,512]{3,2,1,0:T(8,128)} copy(f32[1,1,512,512]{3,2,1,0:T(8,128)S(1)} %bitcast.2) | data formatting | bytes 2097152

commit v5 on v4

--- a/solution.py
+++ b/solution.py
@@ -12,6 +12,7 @@
 RING = 8
 CHUNKS = 4
 SENDS = 8
+REST = 4
 LATE = 5
 ROWS = DV // CHUNKS
 PART = DV // SENDS
@@ -26,6 +27,13 @@
 def gives(i, j):
     even = (i // 4 + j // 4 + i + j) % 2 == 0
     return jnp.logical_or(jnp.logical_and(i > j, jnp.logical_not(even)), jnp.logical_and(i < j, even))
+
+
+def leads(i, j):
+    near = i // RING == j // RING
+    return jnp.logical_or(
+        jnp.logical_and(near, gives(i, j)), jnp.logical_and(jnp.logical_not(near), (i + j) % 2 == 0)
+    )
 
 
 def corner(shape=(HT, HT)):
@@ -156,8 +164,15 @@
     def w_own(h):
         return pltpu.make_async_copy(weighted_ref.at[h], inputs.at[0, h], w_recv.at[0, h])
 
+    lead = leads(i, j)
+    w_first = jnp.logical_or(upper, jnp.logical_and(lead, jnp.logical_not(same)))
+
+    @pl.when(w_first)
+    def _():
+        for h in range(2):
+            w_copy(h).start()
+
     for h in range(2):
-        w_copy(h).start()
 
         @pl.when(lower)
         def _():
@@ -166,6 +181,9 @@
         @pl.when(not_lower)
         def _():
             w_own(h).start()
+
+    def leading(k):
+        return leads(i, half * RING + peer(k))
 
     def f_copy(k):
         to = peer(k)
@@ -186,18 +204,21 @@
     f_own.start()
     x_copy = remote(pack_ref.at[RING], extra.at[me], x_send.at[0], x_recv.at[me], (i, i))
     x_own = pltpu.make_async_copy(pack_ref.at[RING], extra.at[me], x_send.at[1])
-    @pl.when(detours)
-    def _():
+    def send_factors(first):
         for n in range(2):
-            detour(n).start()
-
-    for k in range(1, RING - 2):
-        f_copy(k).start()
-
-    @pl.when(relays)
-    def _():
-        for k in range(RING - 2, RING):
-            f_copy(k).start()
+
+            @pl.when(jnp.logical_and(detours, leading(RING - 2 + n) == first))
+            def _():
+                detour(n).start()
+
+        for k in range(1, RING):
+
+            @pl.when(jnp.logical_and(leading(k) == first, relays if k >= RING - 2 else True))
+            def _():
+                f_copy(k).start()
+
+    send_factors(True)
+    send_factors(False)
 
     @pl.when(jnp.logical_and(same, jnp.logical_not(diag)))
     def _():
@@ -208,6 +229,17 @@
         x_own.start()
 
     total[...] = jnp.zeros_like(total)
+
+    @pl.when(jnp.logical_not(w_first))
+    def _():
+        for k in range(1, RING):
+
+            @pl.when(leading(k))
+            def _():
+                f_copy(k).wait_send()
+
+        for h in range(2):
+            w_copy(h).start()
 
     @pl.when(not_lower)
     def _():
@@ -276,9 +308,11 @@
             await_inputs()
             lax.fori_loop(0, LATE, again, 0)
 
-        @pl.when(jnp.logical_and(relays, k == 1))
-        def _():
-            for n in range(2):
+        for n in range(2):
+            first = leads(i, half * RING + (origin + 2) % 4 * 2 + (core + n) % 2)
+
+            @pl.when(jnp.logical_and(relays, k == jnp.where(first, 1, REST)))
+            def _():
                 detour(n).wait_recv()
                 forward(n).start()
 
@@ -347,7 +381,10 @@
     for h in range(2):
         w_copy(h).wait_send()
     for k in range(1, RING):
-        f_copy(k).wait_send()
+
+        @pl.when(jnp.logical_or(w_first, jnp.logical_not(leading(k))))
+        def _():
+            f_copy(k).wait_send()
 
     @pl.when(relays)
     def _():

time: 87.4 us -> 83.3 us (0.953)
  Pallas kernels: 86.3 us -> 81.9 us
    pallas_call x1, Pallas kernels: 81.9 us -> 77.6 us  [shards(): pl.pallas_call(ladder_kernel, out_shape=jax.ShapeDtypeStruct((DV, DV), jn...]
where the time goes in v5:
time: 83.3 us; the launch traced here: 82.9 us
  Pallas kernels  81.9 us (98%)
  local copies, waits for them, and re-layouts  0.97 us (1%)
    pallas_call x1, Pallas kernels, shards(): pl.pallas_call(ladder_kernel, out_shape=jax.ShapeDtypeStruct((DV, DV), jn...  77.6 us
    pallas_call x1, Pallas kernels, shards(): pl.pallas_call(prep_kernel, out_shape=(pltpu.VMEM((RING + 1, PACK, HT), h...  4.38 us

profile of v5, /device:TPU:5, one launch (start us, length us, event | category | flops | bytes accessed | tf_op | source)
XLA Modules:
  0.0 82.9 jit_solution(7854890093395335785)
XLA Ops:
  0.0 4.4 %prep.1 = (bf16[9,1040,128]{2,1,0:T(8,128)(2,1)S(1)}, bf16[2,512,256]{2,1,0:T(8,128)(2,1)S(1)}) custom-call(s32[16,2,16]{2,1,0:T(2,128)} %bitcast.3, s32[1,1,2,2]{3,2,1,0:T(2,128)} %mask_ref.1, bf16[1,1,512,512]{3,2,1,0:T(8,128)(2,1)} %amp_ref.1, bf16[1,2048,2048]{2,1,0:T(8,128)(2,1)} %chol_ref.1), custom_call_target="tpu_custom_call" | custom-call | tf_op jit(solution)/shard_map/prep/pallas_call | solution.py:420
  4.4 77.6 %ladder.1 = f32[512,512]{1,0:T(8,128)S(1)} custom-call(bf16[9,1040,128]{2,1,0:T(8,128)(2,1)S(1)} %get-tuple-element.7.pack_ref, bf16[2,512,256]{2,1,0:T(8,128)(2,1)S(1)} %get-tuple-element.8.weighted_ref), custom_call_target="tpu_custom_call" | custom-call | tf_op jit(solution)/shard_map/ladder/pallas_call | solution.py:437
  82.0 1.0 %copy.6 = f32[1,1,512,512]{3,2,1,0:T(8,128)} copy(f32[1,1,512,512]{3,2,1,0:T(8,128)S(1)} %bitcast.2) | data formatting | bytes 2097152

commit v6 on v5

--- a/solution.py
+++ b/solution.py
@@ -13,6 +13,7 @@
 CHUNKS = 4
 SENDS = 8
 REST = 4
+SOON = 4
 LATE = 5
 ROWS = DV // CHUNKS
 PART = DV // SENDS
@@ -56,20 +57,16 @@
         t0 = tiles_ref[a, 0, b] * TILE
         t1 = tiles_ref[a, 1, b] * TILE
 
-        def pick(row, col, height, dst, sem):
+        def pick(row, col, width, dst, sem):
             copy = pltpu.make_async_copy(
-                chol_ref.at[0, pl.ds(pl.multiple_of(row, HT), height), pl.ds(pl.multiple_of(col, HT), HT)], dst, sem
+                chol_ref.at[0, pl.ds(pl.multiple_of(row, TILE), TILE), pl.ds(pl.multiple_of(col, HT), width)], dst, sem
             )
             copy.start()
             return copy
 
-        mine = []
-        for n, (t, off) in enumerate(((t0, 0), (t0, HT), (t1, 0), (t1, HT))):
-            mine.append(pick(t + off, t + off, HT, stage.at[s, n], sems.at[s, n]))
-        for n, (row, col, height, at) in enumerate(
-            ((t0, t1, TILE, 0), (t0, t1 + HT, TILE, TILE), (t0, t0 + HT, HT, 2 * TILE), (t1, t1 + HT, HT, 2 * TILE + HT))
-        ):
-            mine.append(pick(row, col, height, pack_ref.at[s, pl.ds(at, height)], sems.at[s, 4 + n]))
+        mine = [pick(t, t, TILE, stage.at[s, n], sems.at[s, n]) for n, t in enumerate((t0, t1))]
+        for n in range(2):
+            mine.append(pick(t0, t1 + n * HT, HT, pack_ref.at[s, pl.ds(n * TILE, TILE)], sems.at[s, 2 + n]))
         copies.append(mine)
         if s == 0:
             raw_copy.start()
@@ -81,15 +78,17 @@
             keep = mask_ref[0, 0, s, t].astype(jnp.float32).astype(jnp.bfloat16)
             weighted_ref[t, pl.ds(s * TILE, TILE), :] = raw[0, 0, pl.ds(s * TILE, TILE), pl.ds(t * TILE, TILE)] * keep
     for s in range(RING + 1):
-        for n in range(4):
+        ends = []
+        for n in range(2):
             copies[s][n].wait()
-        blocks = [stage[s, n].astype(jnp.float32) for n in range(4)]
-        pack_ref[s, 6 * HT : 7 * HT, :] = jnp.where(row <= col, blocks[0], blocks[1]).astype(jnp.bfloat16)
-        pack_ref[s, 7 * HT : 8 * HT, :] = jnp.where(row <= col, blocks[2], blocks[3]).astype(jnp.bfloat16)
-        ends = [jnp.sum(jnp.where(row == col, blocks[n], 0.0), axis=0, keepdims=True) for n in (1, 3)]
+            pack_ref[s, (4 + n) * HT : (5 + n) * HT, :] = stage[s, n, :HT, HT:]
+            first = stage[s, n, :HT, :HT].astype(jnp.float32)
+            second = stage[s, n, HT:, HT:].astype(jnp.float32)
+            pack_ref[s, (6 + n) * HT : (7 + n) * HT, :] = jnp.where(row <= col, first, second).astype(jnp.bfloat16)
+            ends.append(jnp.sum(jnp.where(row == col, second, 0.0), axis=0, keepdims=True))
         pack_ref[s, 8 * HT :, :] = jnp.where(line == 0, ends[0], ends[1]).astype(jnp.bfloat16)
     for s in range(RING + 1):
-        for n in range(4, 8):
+        for n in range(2, 4):
             copies[s][n].wait()
 
 
@@ -166,6 +165,7 @@
 
     lead = leads(i, j)
     w_first = jnp.logical_or(upper, jnp.logical_and(lead, jnp.logical_not(same)))
+    w_held = jnp.logical_not(w_first)
 
     @pl.when(w_first)
     def _():
@@ -230,7 +230,7 @@
 
     total[...] = jnp.zeros_like(total)
 
-    @pl.when(jnp.logical_not(w_first))
+    @pl.when(w_held)
     def _():
         for k in range(1, RING):
 
@@ -282,31 +282,25 @@
                 inner[...], factor[which, :, cols], preferred_element_type=jnp.float32
             )
 
-    def await_inputs():
-        for h in range(2):
-            w_copy(h).wait_recv()
-
-        @pl.when(lower)
+    def again(n, carry):
+        add(1, n + RING * dflag)
+        return carry
+
+    def step(k, carry):
+        slot = peer(k)
+
+        @pl.when(k == LATE)
+        def _():
+            for h in range(2):
+                w_copy(h).wait_recv()
+            lax.fori_loop(0, LATE, again, 0)
+
+        @pl.when(jnp.logical_and(lower, k == SOON))
         def _():
             for h in range(2):
                 w_more(h).wait_recv()
-
-    def again(n, carry):
-        add(1, n + RING * dflag)
-
-        @pl.when(lower)
-        def _():
-            add(0, n)
-
-        return carry
-
-    def step(k, carry):
-        slot = peer(k)
-
-        @pl.when(k == LATE)
-        def _():
-            await_inputs()
-            lax.fori_loop(0, LATE, again, 0)
+            for n in range(SOON):
+                add(0, n)
 
         for n in range(2):
             first = leads(i, half * RING + (origin + 2) % 4 * 2 + (core + n) % 2)
@@ -330,7 +324,7 @@
 
             build(extra, slot, k + RING)
 
-        @pl.when(not_lower)
+        @pl.when(jnp.logical_or(not_lower, k >= SOON))
         def _():
             add(0, k)
 
@@ -382,7 +376,7 @@
         w_copy(h).wait_send()
     for k in range(1, RING):
 
-        @pl.when(jnp.logical_or(w_first, jnp.logical_not(leading(k))))
+        @pl.when(jnp.logical_not(jnp.logical_and(w_held, leading(k))))
         def _():
             f_copy(k).wait_send()
 
@@ -426,9 +420,9 @@
         in_specs=[smem, smem, hbm, hbm],
         out_specs=(vmem, vmem),
         scratch_shapes=[
-            pltpu.VMEM((RING + 1, 4, HT, HT), half),
+            pltpu.VMEM((RING + 1, 2, TILE, TILE), half),
             pltpu.VMEM((1, 1, DV, DV), half),
-            dma((RING + 1, 8)),
+            dma((RING + 1, 4)),
             dma,
         ],
         compiler_params=pltpu.CompilerParams(vmem_limit_bytes=56 << 20),

time: 83.3 us -> 82 us (0.984)
  Pallas kernels: 81.9 us -> 80.4 us
    pallas_call x1, Pallas kernels: 77.6 us -> 76 us  [shards(): pl.pallas_call(ladder_kernel, out_shape=jax.ShapeDtypeStruct((DV, DV), jn...]
where the time goes in v6:
time: 82 us; the launch traced here: 81.4 us
  Pallas kernels  80.4 us (98%)
  local copies, waits for them, and re-layouts  0.97 us (1%)
    pallas_call x1, Pallas kernels, shards(): pl.pallas_call(ladder_kernel, out_shape=jax.ShapeDtypeStruct((DV, DV), jn...  76 us
    pallas_call x1, Pallas kernels, shards(): pl.pallas_call(prep_kernel, out_shape=(pltpu.VMEM((RING + 1, PACK, HT), h...  4.42 us

profile of v6, /device:TPU:5, one launch (start us, length us, event | category | flops | bytes accessed | tf_op | source)
XLA Modules:
  0.0 81.4 jit_solution(17285465626422755771)
XLA Ops:
  0.0 4.4 %prep.1 = (bf16[9,1040,128]{2,1,0:T(8,128)(2,1)S(1)}, bf16[2,512,256]{2,1,0:T(8,128)(2,1)S(1)}) custom-call(s32[16,2,16]{2,1,0:T(2,128)} %bitcast.3, s32[1,1,2,2]{3,2,1,0:T(2,128)} %mask_ref.1, bf16[1,1,512,512]{3,2,1,0:T(8,128)(2,1)} %amp_ref.1, bf16[1,2048,2048]{2,1,0:T(8,128)(2,1)} %chol_ref.1), custom_call_target="tpu_custom_call" | custom-call | tf_op jit(solution)/shard_map/prep/pallas_call | solution.py:414
  4.4 76.0 %ladder.1 = f32[512,512]{1,0:T(8,128)S(1)} custom-call(bf16[9,1040,128]{2,1,0:T(8,128)(2,1)S(1)} %get-tuple-element.7.pack_ref, bf16[2,512,256]{2,1,0:T(8,128)(2,1)S(1)} %get-tuple-element.8.weighted_ref), custom_call_target="tpu_custom_call" | custom-call | tf_op jit(solution)/shard_map/ladder/pallas_call | solution.py:431
  80.4 1.0 %copy.6 = f32[1,1,512,512]{3,2,1,0:T(8,128)} copy(f32[1,1,512,512]{3,2,1,0:T(8,128)S(1)} %bitcast.2) | data formatting | bytes 2097152

commit v7 on v6

--- a/solution.py
+++ b/solution.py
@@ -12,7 +12,7 @@
 RING = 8
 CHUNKS = 4
 SENDS = 8
-REST = 4
+REST = 5
 SOON = 4
 LATE = 5
 ROWS = DV // CHUNKS

time: 82 us -> 80.9 us (0.987)
  no operation moved by 1% of the time
where the time goes in v7:
time: 80.9 us; the launch traced here: 80.7 us
  Pallas kernels  79.7 us (99%)
  local copies, waits for them, and re-layouts  0.97 us (1%)
    pallas_call x1, Pallas kernels, shards(): pl.pallas_call(ladder_kernel, out_shape=jax.ShapeDtypeStruct((DV, DV), jn...  75.4 us
    pallas_call x1, Pallas kernels, shards(): pl.pallas_call(prep_kernel, out_shape=(pltpu.VMEM((RING + 1, PACK, HT), h...  4.32 us

profile of v7, /device:TPU:5, one launch (start us, length us, event | category | flops | bytes accessed | tf_op | source)
XLA Modules:
  0.0 80.7 jit_solution(5943308699629293742)
XLA Ops:
  0.0 4.3 %prep.1 = (bf16[9,1040,128]{2,1,0:T(8,128)(2,1)S(1)}, bf16[2,512,256]{2,1,0:T(8,128)(2,1)S(1)}) custom-call(s32[16,2,16]{2,1,0:T(2,128)} %bitcast.3, s32[1,1,2,2]{3,2,1,0:T(2,128)} %mask_ref.1, bf16[1,1,512,512]{3,2,1,0:T(8,128)(2,1)} %amp_ref.1, bf16[1,2048,2048]{2,1,0:T(8,128)(2,1)} %chol_ref.1), custom_call_target="tpu_custom_call" | custom-call | tf_op jit(solution)/shard_map/prep/pallas_call | solution.py:414
  4.3 75.4 %ladder.1 = f32[512,512]{1,0:T(8,128)S(1)} custom-call(bf16[9,1040,128]{2,1,0:T(8,128)(2,1)S(1)} %get-tuple-element.7.pack_ref, bf16[2,512,256]{2,1,0:T(8,128)(2,1)S(1)} %get-tuple-element.8.weighted_ref), custom_call_target="tpu_custom_call" | custom-call | tf_op jit(solution)/shard_map/ladder/pallas_call | solution.py:431
  79.8 1.0 %copy.6 = f32[1,1,512,512]{3,2,1,0:T(8,128)} copy(f32[1,1,512,512]{3,2,1,0:T(8,128)S(1)} %bitcast.2) | data formatting | bytes 2097152

commit v8 on v7

--- a/solution.py
+++ b/solution.py
@@ -45,7 +45,14 @@
     i = lax.axis_index("orow")
     half = lax.axis_index("ocol") // RING
     raw_copy = pltpu.make_async_copy(amp_ref, raw, raw_sem)
-    copies = []
+    def pick(row, col, width, dst, sem):
+        copy = pltpu.make_async_copy(
+            chol_ref.at[0, pl.ds(pl.multiple_of(row, TILE), TILE), pl.ds(pl.multiple_of(col, HT), width)], dst, sem
+        )
+        copy.start()
+        return copy
+
+    copies, corners = [], []
     for s in range(RING + 1):
         if s < RING:
             j = half * RING + s
@@ -57,26 +64,15 @@
         t0 = tiles_ref[a, 0, b] * TILE
         t1 = tiles_ref[a, 1, b] * TILE
 
-        def pick(row, col, width, dst, sem):
-            copy = pltpu.make_async_copy(
-                chol_ref.at[0, pl.ds(pl.multiple_of(row, TILE), TILE), pl.ds(pl.multiple_of(col, HT), width)], dst, sem
-            )
-            copy.start()
-            return copy
-
         mine = [pick(t, t, TILE, stage.at[s, n], sems.at[s, n]) for n, t in enumerate((t0, t1))]
-        for n in range(2):
-            mine.append(pick(t0, t1 + n * HT, HT, pack_ref.at[s, pl.ds(n * TILE, TILE)], sems.at[s, 2 + n]))
         copies.append(mine)
-        if s == 0:
-            raw_copy.start()
+        corners.append((t0, t1))
+    raw_copy.start()
+    for s, (t0, t1) in enumerate(corners):
+        for n in range(2):
+            copies[s].append(pick(t0, t1 + n * HT, HT, pack_ref.at[s, pl.ds(n * TILE, TILE)], sems.at[s, 2 + n]))
     row, col = corner()
     line = lax.broadcasted_iota(jnp.int32, (16, HT), 0)
-    raw_copy.wait()
-    for s in range(2):
-        for t in range(2):
-            keep = mask_ref[0, 0, s, t].astype(jnp.float32).astype(jnp.bfloat16)
-            weighted_ref[t, pl.ds(s * TILE, TILE), :] = raw[0, 0, pl.ds(s * TILE, TILE), pl.ds(t * TILE, TILE)] * keep
     for s in range(RING + 1):
         ends = []
         for n in range(2):
@@ -87,6 +83,11 @@
             pack_ref[s, (6 + n) * HT : (7 + n) * HT, :] = jnp.where(row <= col, first, second).astype(jnp.bfloat16)
             ends.append(jnp.sum(jnp.where(row == col, second, 0.0), axis=0, keepdims=True))
         pack_ref[s, 8 * HT :, :] = jnp.where(line == 0, ends[0], ends[1]).astype(jnp.bfloat16)
+    raw_copy.wait()
+    for s in range(2):
+        for t in range(2):
+            keep = mask_ref[0, 0, s, t].astype(jnp.float32).astype(jnp.bfloat16)
+            weighted_ref[t, pl.ds(s * TILE, TILE), :] = raw[0, 0, pl.ds(s * TILE, TILE), pl.ds(t * TILE, TILE)] * keep
     for s in range(RING + 1):
         for n in range(2, 4):
             copies[s][n].wait()

time: 80.9 us -> 80.3 us (level)
  no operation moved by 1% of the time
where the time goes in v8:
time: 80.3 us; the launch traced here: 80.1 us
  Pallas kernels  79.1 us (99%)
  local copies, waits for them, and re-layouts  0.97 us (1%)
    pallas_call x1, Pallas kernels, shards(): pl.pallas_call(ladder_kernel, out_shape=jax.ShapeDtypeStruct((DV, DV), jn...  75.4 us
    pallas_call x1, Pallas kernels, shards(): pl.pallas_call(prep_kernel, out_shape=(pltpu.VMEM((RING + 1, PACK, HT), h...  3.76 us

profile of v8, /device:TPU:5, one launch (start us, length us, event | category | flops | bytes accessed | tf_op | source)
XLA Modules:
  0.0 80.1 jit_solution(11361506606482945713)
XLA Ops:
  0.0 3.8 %prep.1 = (bf16[9,1040,128]{2,1,0:T(8,128)(2,1)S(1)}, bf16[2,512,256]{2,1,0:T(8,128)(2,1)S(1)}) custom-call(s32[16,2,16]{2,1,0:T(2,128)} %bitcast.3, s32[1,1,2,2]{3,2,1,0:T(2,128)} %mask_ref.1, bf16[1,1,512,512]{3,2,1,0:T(8,128)(2,1)} %amp_ref.1, bf16[1,2048,2048]{2,1,0:T(8,128)(2,1)} %chol_ref.1), custom_call_target="tpu_custom_call" | custom-call | tf_op jit(solution)/shard_map/prep/pallas_call | solution.py:415
  3.8 75.4 %ladder.1 = f32[512,512]{1,0:T(8,128)S(1)} custom-call(bf16[9,1040,128]{2,1,0:T(8,128)(2,1)S(1)} %get-tuple-element.7.pack_ref, bf16[2,512,256]{2,1,0:T(8,128)(2,1)S(1)} %get-tuple-element.8.weighted_ref), custom_call_target="tpu_custom_call" | custom-call | tf_op jit(solution)/shard_map/ladder/pallas_call | solution.py:432
  79.1 1.0 %copy.6 = f32[1,1,512,512]{3,2,1,0:T(8,128)} copy(f32[1,1,512,512]{3,2,1,0:T(8,128)S(1)} %bitcast.2) | data formatting | bytes 2097152

commit v9 on v8

--- a/solution.py
+++ b/solution.py
@@ -212,7 +212,7 @@
             def _():
                 detour(n).start()
 
-        for k in range(1, RING):
+        for k in (6, 7, 2, 3, 4, 5, 1):
 
             @pl.when(jnp.logical_and(leading(k) == first, relays if k >= RING - 2 else True))
             def _():

time: 80.3 us -> 80.3 us (level)
  no operation moved by 1% of the time
where the time goes in v9:
time: 80.3 us; the launch traced here: 80.1 us
  Pallas kernels  79.1 us (99%)
  local copies, waits for them, and re-layouts  0.97 us (1%)
    pallas_call x1, Pallas kernels, shards(): pl.pallas_call(ladder_kernel, out_shape=jax.ShapeDtypeStruct((DV, DV), jn...  75.4 us
    pallas_call x1, Pallas kernels, shards(): pl.pallas_call(prep_kernel, out_shape=(pltpu.VMEM((RING + 1, PACK, HT), h...  3.73 us

profile of v9, /device:TPU:5, one launch (start us, length us, event | category | flops | bytes accessed | tf_op | source)
XLA Modules:
  0.0 80.1 jit_solution(2439713141662742394)
XLA Ops:
  0.0 3.7 %prep.1 = (bf16[9,1040,128]{2,1,0:T(8,128)(2,1)S(1)}, bf16[2,512,256]{2,1,0:T(8,128)(2,1)S(1)}) custom-call(s32[16,2,16]{2,1,0:T(2,128)} %bitcast.3, s32[1,1,2,2]{3,2,1,0:T(2,128)} %mask_ref.1, bf16[1,1,512,512]{3,2,1,0:T(8,128)(2,1)} %amp_ref.1, bf16[1,2048,2048]{2,1,0:T(8,128)(2,1)} %chol_ref.1), custom_call_target="tpu_custom_call" | custom-call | tf_op jit(solution)/shard_map/prep/pallas_call | solution.py:415
  3.7 75.4 %ladder.1 = f32[512,512]{1,0:T(8,128)S(1)} custom-call(bf16[9,1040,128]{2,1,0:T(8,128)(2,1)S(1)} %get-tuple-element.7.pack_ref, bf16[2,512,256]{2,1,0:T(8,128)(2,1)S(1)} %get-tuple-element.8.weighted_ref), custom_call_target="tpu_custom_call" | custom-call | tf_op jit(solution)/shard_map/ladder/pallas_call | solution.py:432
  79.2 1.0 %copy.6 = f32[1,1,512,512]{3,2,1,0:T(8,128)} copy(f32[1,1,512,512]{3,2,1,0:T(8,128)S(1)} %bitcast.2) | data formatting | bytes 2097152
